TPU v7x, 32 devices: a whole 2x2x4 slice. The times are simulated.
32 devices in a mesh: dp: 4 (over z), vocab: 8 (over y, x, core).
Axes of the slice: x: 2, y: 2, z: 4, core: 2. Of those that a mesh axis runs over, the one named last changes fastest.
Arguments:
- token_ids: int32 [8192], P(('dp', 'vocab')), may hold values from 0 to 152063, as said below
- token_count: int32 [32], P(('dp', 'vocab')), may hold values from 16 to 256
- out_grads: bfloat16 [8192, 5120], P(('dp', 'vocab')), may hold values from -18 to 18
- master_rows: float32 [4096, 5120], P('vocab', 'dp'), may hold values from -0.8 to 0.8
- first_moment: float32 [4096, 5120], P('vocab', 'dp'), may hold values from -4 to 4
- second_moment: float32 [4096, 5120], P('vocab', 'dp'), may hold values from 0.001 to 1
Outputs:
- new_master: float32 [4096, 5120], P('vocab', 'dp')
- new_first: float32 [4096, 5120], P('vocab', 'dp')
- new_second: float32 [4096, 5120], P('vocab', 'dp')
- table_rows: bfloat16 [4096, 5120], P('vocab')
Inputs may be any that keep to these rules, and one draw needn't show every extreme that they name: `token_ids`: within each block of 256 slots, among the live slots (the first token_count of the block) at most 8 have ids in the new rows j * 512 + 147968 to (j + 1) * 512 + 147967 for any one j, and for some j exactly 8 in every block. Slots past token_count hold ids of new rows that are to be ignored.
All inputs are finite; a program needn't handle non-finite values.
Results may differ from a plain program's by a relative error of at most 0.001.
Values may be sent and summed in bfloat16 or wider, within the bound.
A program may use at most 64 MiB of HBM per device.

v0:
```python
import jax
import jax.numpy as jnp
from jax import lax
from jax.sharding import PartitionSpec as P

VOCAB = 152064
CAP = 8


beta_one = 0.9
beta_two = 0.999
corr_one = 1.0 - 0.9**10
corr_two = 1.0 - 0.999**10
learn_rate = 0.01
epsilon = 1e-08


def body(token_ids, token_count, out_grads, master_rows, first_moment, second_moment):
    owners = lax.axis_size("vocab")
    groups = lax.axis_size("dp")
    rows_own = master_rows.shape[0]
    tok_slots = token_ids.shape[0]
    first_new = VOCAB - rows_own * owners
    position = jnp.arange(tok_slots)
    is_live = (position < token_count[0]) & (token_ids >= first_new)
    new_index = token_ids - first_new
    owner_of = new_index // rows_own
    row_in_owner = new_index % rows_own
    belongs = (owner_of[:, None] == jnp.arange(owners)[None, :]) & is_live[:, None]
    ranking = jnp.cumsum(belongs.astype(jnp.int32), axis=0) - 1
    my_rank = jnp.sum(jnp.where(belongs, ranking, 0), axis=1)
    slot_index = jnp.where(is_live, owner_of * CAP + my_rank, -1)
    placing = jnp.arange(owners * CAP)[:, None] == slot_index[None, :]
    outgoing = jnp.dot(
        placing.astype(jnp.bfloat16), out_grads, preferred_element_type=jnp.float32
    ).astype(jnp.bfloat16)
    slot_row = jnp.max(jnp.where(placing, row_in_owner[None, :], -1), axis=1)
    upper_part = jnp.where(slot_row >= 0, slot_row // 16, -1)
    lower_part = jnp.where(slot_row >= 0, slot_row % 16, 0)
    row_pairs = jnp.stack([upper_part, lower_part], axis=1).astype(jnp.bfloat16)
    tiled_pairs = jnp.tile(row_pairs, (1, groups))
    split_grads, split_pairs = (
        lax.all_to_all(outgoing, "dp", split_axis=1, concat_axis=0, tiled=True),
        lax.all_to_all(tiled_pairs, "dp", split_axis=1, concat_axis=0, tiled=True),
    )
    split_grads = split_grads.reshape(groups, owners * CAP, split_grads.shape[1])
    split_pairs = split_pairs.reshape(groups, owners * CAP, 2)
    arrived, arrived_pairs = (
        lax.all_to_all(split_grads, "vocab", split_axis=1, concat_axis=0, tiled=True),
        lax.all_to_all(split_pairs, "vocab", split_axis=1, concat_axis=0, tiled=True),
    )
    arrived = arrived.reshape(-1, arrived.shape[2])
    arrived_pairs = arrived_pairs.reshape(-1, 2).astype(jnp.float32)
    decoded = arrived_pairs[:, 0] * 16.0 + arrived_pairs[:, 1]
    selector = decoded[None, :] == jnp.arange(rows_own, dtype=jnp.float32)[:, None]
    gradient = jnp.dot(selector.astype(jnp.bfloat16), arrived, preferred_element_type=jnp.float32)
    new_first = beta_one * first_moment + (1.0 - beta_one) * gradient
    new_second = beta_two * second_moment + (1.0 - beta_two) * gradient * gradient
    update = new_first / corr_one / (jnp.sqrt(new_second / corr_two) + epsilon)
    new_master = master_rows - learn_rate * update
    table_rows = lax.all_gather(new_master.astype(jnp.bfloat16), "dp", axis=1, tiled=True)
    return (new_master, new_first, new_second, table_rows)


def solution(mesh):
    return jax.shard_map(
        body,
        mesh=mesh,
        in_specs=(
            P(("dp", "vocab")),
            P(("dp", "vocab")),
            P(("dp", "vocab"), None),
            P("vocab", "dp"),
            P("vocab", "dp"),
            P("vocab", "dp"),
        ),
        out_specs=(P("vocab", "dp"), P("vocab", "dp"), P("vocab", "dp"), P("vocab", None)),
        check_vma=False,
    )
```

profile of v0, /device:TPU:0, one launch (start us, length us, event | category | flops | bytes accessed | tf_op | source)
XLA Modules:
  0.0 184.4 jit_solution(8135836550928736007)
XLA Ops:
  7.2 0.0 copy-start
  8.0 0.7 and_select_fusion.2
  8.7 0.7 fusion.14
  9.4 0.7 compare_and_fusion
  10.0 0.6 reduce-window.6
  10.6 0.2 slice_reduce_fusion
  10.9 0.1 fusion.4
  11.0 0.7 add_select_fusion
  11.7 0.1 select_reduce_fusion
  11.8 0.6 tile.2
  12.4 6.3 %all-to-all-start = ((bf16[64,4,2]{0,2,1:T(2,128)(2,1)}), bf16[64,4,2]{0,2,1:T(2,128)(2,1)S(1)}, u32[]{:S(2)}, u32[]{:S(2)}) async-start(bf16[64,4,2]{0,2,1:T(2,128)(2,1)} %tile.2), calls=%async_computation | async-start | bytes 4096 | tf_op jit(solution)/shard_map/all_to_all | solution.py:44
  18.8 0.0 copy-done
  18.8 0.6 convolution_convert_fusion
  19.3 0.9 copy.45
  20.2 4.0 %all-to-all-done = bf16[64,4,2]{0,2,1:T(2,128)(2,1)S(1)} async-done(((bf16[64,4,2]{0,2,1:T(2,128)(2,1)}), bf16[64,4,2]{0,2,1:T(2,128)(2,1)S(1)}, u32[]{:S(2)}, u32[]{:S(2)}) %all-to-all-start) | async-done | bytes 1056 | tf_op jit(solution)/shard_map/all_to_all | solution.py:44
  24.3 3.5 %all-to-all-start.2 = ((bf16[64,4,1280]{2,0,1:T(8,128)(2,1)}), bf16[64,4,1280]{2,0,1:T(8,128)(2,1)S(1)}, u32[]{:S(2)}, u32[]{:S(2)}) async-start(bf16[64,4,1280]{2,0,1:T(8,128)(2,1)} %bitcast.52), calls=%async_computation.2 | async-start | bytes 1310720 | tf_op jit(solution)/shard_map/all_to_all | solution.py:43
  27.7 0.7 copy.34
  28.5 15.4 %all-to-all-done.2 = bf16[64,4,1280]{2,0,1:T(8,128)(2,1)S(1)} async-done(((bf16[64,4,1280]{2,0,1:T(8,128)(2,1)}), bf16[64,4,1280]{2,0,1:T(8,128)(2,1)S(1)}, u32[]{:S(2)}, u32[]{:S(2)}) %all-to-all-start.2) | async-done | bytes 655392 | tf_op jit(solution)/shard_map/all_to_all | solution.py:43
  43.9 3.7 %all-to-all-start.1 = ((bf16[4,64,2]{0,2,1:T(2,128)(2,1)}), bf16[4,64,2]{0,2,1:T(2,128)(2,1)S(1)}, u32[]{:S(2)}, u32[]{:S(2)}) async-start(bf16[4,64,2]{0,2,1:T(2,128)(2,1)} %copy.34), calls=%async_computation.1 | async-start | bytes 65536 | tf_op jit(solution)/shard_map/all_to_all | solution.py:50
  47.6 1.3 copy.39
  48.9 3.5 %all-to-all-done.1 = bf16[4,64,2]{0,2,1:T(2,128)(2,1)S(1)} async-done(((bf16[4,64,2]{0,2,1:T(2,128)(2,1)}), bf16[4,64,2]{0,2,1:T(2,128)(2,1)S(1)}, u32[]{:S(2)}, u32[]{:S(2)}) %all-to-all-start.1) | async-done | bytes 1056 | tf_op jit(solution)/shard_map/all_to_all | solution.py:50
  52.4 3.5 %all-to-all-start.3 = ((bf16[4,64,1280]{2,0,1:T(4,128)(2,1)}), bf16[4,64,1280]{2,0,1:T(4,128)(2,1)S(1)}, u32[]{:S(2)}, u32[]{:S(2)}) async-start(bf16[4,64,1280]{2,0,1:T(4,128)(2,1)} %copy.39), calls=%async_computation.3 | async-start | bytes 1310720 | tf_op jit(solution)/shard_map/all_to_all | solution.py:49
  56.0 0.0 all-gather.2.cloned.1.call-start
  56.0 0.1 copy.35
  56.1 0.1 reshape.169
  56.2 0.1 reshape.168
  56.4 10.7 %all-to-all-done.3 = bf16[4,64,1280]{2,0,1:T(4,128)(2,1)S(1)} async-done(((bf16[4,64,1280]{2,0,1:T(4,128)(2,1)}), bf16[4,64,1280]{2,0,1:T(4,128)(2,1)S(1)}, u32[]{:S(2)}, u32[]{:S(2)}) %all-to-all-start.3) | async-done | bytes 655392 | tf_op jit(solution)/shard_map/all_to_all | solution.py:49
  67.0 0.0 copy-start.1
  67.0 0.1 copy.46
  67.2 1.6 copy-done.1
  68.8 8.2 %fusion.10 = (bf16[512,1280]{1,0:T(8,128)(2,1)}, f32[512,1280]{1,0:T(8,128)}, f32[512,1280]{1,0:T(8,128)}, f32[512,1280]{1,0:T(8,128)}) fusion(f32[512,1280]{1,0:T(8,128)S(1)} %copy-done.1, f32[512,1280]{1,0:T(8,128)} %param.10, f32[512,1280]{1,0:T(8,128)} %param.11, bf16[256,1280]{1,0:T(8,128)(2,1)S(1)} %bitcast.55, f32[256]{0:T(256)S(1)} %bitcast.59), kind=kOutput, calls=%fused_computation.43 | convolution fusion | flops 344850432 | bytes 17695744 | tf_op jit(solution)/shard_map/dot_general | solution.py:56
  77.0 0.0 all-gather.2.cloned.1.call-update
  77.0 95.4 %all-gather.2.cloned.1.call-done = bf16[512,5120]{1,0:T(8,128)(2,1)} async-done(((bf16[512,1280]{1,0:T(8,128)(2,1)}), bf16[512,5120]{1,0:T(8,128)(2,1)}) %all-gather.2.cloned.1.call-update) | async-done | bytes 5242896 | tf_op jit(solution)/shard_map/all_gather | solution.py:61
  172.4 5.2 %copy.49 = bf16[512,5120]{1,0:T(8,128)(2,1)} copy(bf16[512,5120]{1,0:T(8,128)(2,1)} %all-gather.2.cloned.1.call-done) | data formatting | bytes 10485760
  (9 shorter events, 0.2 us)
Async XLA Ops:
  7.2 11.6 %copy-start = (bf16[256,5120]{1,0:T(8,128)(2,1)S(1)}, bf16[256,5120]{1,0:T(8,128)(2,1)}, u32[]{:S(2)}) copy-start(bf16[256,5120]{1,0:T(8,128)(2,1)} %param.8) | copy-start | bytes 7864324
  12.4 11.8 %all-to-all-start = ((bf16[64,4,2]{0,2,1:T(2,128)(2,1)}), bf16[64,4,2]{0,2,1:T(2,128)(2,1)S(1)}, u32[]{:S(2)}, u32[]{:S(2)}) async-start(bf16[64,4,2]{0,2,1:T(2,128)(2,1)} %tile.2), calls=%async_computation | async-start | bytes 4096 | tf_op jit(solution)/shard_map/all_to_all | solution.py:44
  24.3 19.6 %all-to-all-start.2 = ((bf16[64,4,1280]{2,0,1:T(8,128)(2,1)}), bf16[64,4,1280]{2,0,1:T(8,128)(2,1)S(1)}, u32[]{:S(2)}, u32[]{:S(2)}) async-start(bf16[64,4,1280]{2,0,1:T(8,128)(2,1)} %bitcast.52), calls=%async_computation.2 | async-start | bytes 1310720 | tf_op jit(solution)/shard_map/all_to_all | solution.py:43
  43.9 8.6 %all-to-all-start.1 = ((bf16[4,64,2]{0,2,1:T(2,128)(2,1)}), bf16[4,64,2]{0,2,1:T(2,128)(2,1)S(1)}, u32[]{:S(2)}, u32[]{:S(2)}) async-start(bf16[4,64,2]{0,2,1:T(2,128)(2,1)} %copy.34), calls=%async_computation.1 | async-start | bytes 65536 | tf_op jit(solution)/shard_map/all_to_all | solution.py:50
  52.4 14.6 %all-to-all-start.3 = ((bf16[4,64,1280]{2,0,1:T(4,128)(2,1)}), bf16[4,64,1280]{2,0,1:T(4,128)(2,1)S(1)}, u32[]{:S(2)}, u32[]{:S(2)}) async-start(bf16[4,64,1280]{2,0,1:T(4,128)(2,1)} %copy.39), calls=%async_computation.3 | async-start | bytes 1310720 | tf_op jit(solution)/shard_map/all_to_all | solution.py:49
  56.0 116.4 %all-gather.2.cloned.1.call-start = ((), (), s32[]{:S(2)}) async-start(), calls=%async_computation.4 | async-start | bytes 6553600 | tf_op jit(solution)/shard_map/all_gather | solution.py:61
  67.0 1.7 copy-start.1
Sparse Core Ops, SparseCore 0:
  77.1 95.2 all-gather.1
where the time goes:
time: 185 us; the launch traced here: 184 us
  waiting for transfers between devices  129 us (70%)
  starting transfers between devices  17.1 us (9%)
  between operations  14.9 us (8%)
  local copies, waits for them, and re-layouts  11 us (6%)
  matrix products  8.76 us (5%)
  other arithmetic  3.62 us (2%)
    all_gather x1, waiting for transfers between devices, body(): lax.all_gather(new_master.astype(jnp.bfloat16), 'dp', axis=1, tiled=True)  95.4 us
    all_to_all x1, waiting for transfers between devices, body(): lax.all_to_all(outgoing, 'dp', split_axis=1, concat_axis=0, tiled=True)  15.4 us
    all_to_all x1, waiting for transfers between devices, body(): lax.all_to_all(split_grads, 'vocab', split_axis=1, concat_axis=0, tiled=T...  10.7 us
    dot_general x1, matrix products, body(): jnp.dot(selector.astype(jnp.bfloat16), arrived, preferred_element_type=jn...  8.19 us
    unnamed x5, local copies, waits for them, and re-layouts  6.81 us
    all_to_all x1, starting transfers between devices, body(): lax.all_to_all(tiled_pairs, 'dp', split_axis=1, concat_axis=0, tiled=True)  6.35 us
    all_to_all x1, waiting for transfers between devices, body(): lax.all_to_all(tiled_pairs, 'dp', split_axis=1, concat_axis=0, tiled=True)  4.04 us
    all_to_all x1, starting transfers between devices, body(): lax.all_to_all(split_pairs, 'vocab', split_axis=1, concat_axis=0, tiled=T...  3.72 us
  transfers between devices with their start and end apart: 5, of which 5 were waited for; matrix products, arithmetic and copies ran while one was open for 2% of the time, Pallas kernels for 0%

commit v1 on v0

v1 whole, which is shorter than its diff:
```python
import functools

import jax
import jax.numpy as jnp
from jax import lax
from jax.experimental import pallas as pl
from jax.experimental.pallas import tpu as pltpu
from jax.sharding import PartitionSpec as P

VOCAB = 152064
CAP = 8
LANES = 128
CHUNKS = 8
MESH = pl.DeviceIdType.MESH


beta_one = 0.9
beta_two = 0.999
corr_one = 1.0 - 0.9**10
corr_two = 1.0 - 0.999**10
learn_rate = 0.01
epsilon = 1e-08


def exchange_kernel(groups, owners, out_ref, arr_ref, send_sem, recv_sem, own_sem):
    my_dp, my_vocab = lax.axis_index("dp"), lax.axis_index("vocab")
    total = groups * owners
    me = my_dp * owners + my_vocab
    barrier = pltpu.get_barrier_semaphore()

    def target(k):
        other = lax.rem(me + k, total)
        return other // owners, lax.rem(other, owners)

    def greet(k, carry):
        pl.semaphore_signal(barrier, inc=1, device_id=target(k), device_id_type=MESH)
        return carry

    lax.fori_loop(1, total, greet, 0)
    pl.semaphore_wait(barrier, total - 1)

    own = pltpu.make_async_copy(out_ref.at[my_dp, my_vocab], arr_ref.at[me], own_sem)
    own.start()

    def copy(k):
        to_dp, to_vocab = target(k)
        return pltpu.make_async_remote_copy(
            src_ref=out_ref.at[to_dp, to_vocab],
            dst_ref=arr_ref.at[me],
            send_sem=send_sem.at[k],
            recv_sem=recv_sem.at[k],
            device_id=(to_dp, to_vocab),
            device_id_type=MESH,
        )

    def send(k, carry):
        copy(k).start()
        return carry

    lax.fori_loop(1, total, send, 0)

    def finish(k, carry):
        copy(k).wait_send()
        sender = lax.rem(me - k + total, total)
        pltpu.make_async_remote_copy(
            src_ref=out_ref.at[my_dp, my_vocab],
            dst_ref=arr_ref.at[sender],
            send_sem=send_sem.at[k],
            recv_sem=recv_sem.at[k],
            device_id=target(k),
            device_id_type=MESH,
        ).wait_recv()
        return carry

    lax.fori_loop(1, total, finish, 0)
    own.wait()


def exchange(outgoing):
    groups, owners, cap, width = outgoing.shape
    total = groups * owners
    return pl.pallas_call(
        functools.partial(exchange_kernel, groups, owners),
        out_shape=jax.ShapeDtypeStruct((total, cap, width), outgoing.dtype),
        in_specs=[pl.BlockSpec(memory_space=pltpu.VMEM)],
        out_specs=pl.BlockSpec(memory_space=pltpu.VMEM),
        scratch_shapes=[
            pltpu.SemaphoreType.DMA((total,)),
            pltpu.SemaphoreType.DMA((total,)),
            pltpu.SemaphoreType.DMA,
        ],
        compiler_params=pltpu.CompilerParams(collective_id=0, has_side_effects=True),
        name="exchange",
    )(outgoing)


def gather_kernel(groups, block_ref, table_ref, left_sem, right_sem, recv_sem, own_sem):
    my_dp = lax.axis_index("dp")
    rows, columns = block_ref.shape
    step_rows = rows // CHUNKS
    barrier = pltpu.get_barrier_semaphore()
    has_left, has_right = my_dp > 0, my_dp < groups - 1

    @pl.when(has_left)
    def _():
        pl.semaphore_signal(barrier, inc=1, device_id={"dp": my_dp - 1}, device_id_type=MESH)

    @pl.when(has_right)
    def _():
        pl.semaphore_signal(barrier, inc=1, device_id={"dp": my_dp + 1}, device_id_type=MESH)

    pl.semaphore_wait(barrier, has_left.astype(jnp.int32) + has_right.astype(jnp.int32))

    def place(block, chunk):
        start = pl.multiple_of(block * columns, LANES)
        return table_ref.at[pl.ds(chunk * step_rows, step_rows), pl.ds(start, columns)]

    own = pltpu.make_async_copy(
        block_ref, table_ref.at[:, pl.ds(pl.multiple_of(my_dp * columns, LANES), columns)], own_sem
    )
    own.start()

    def copy(block, chunk, step, sem, to_dp):
        source = (
            block_ref.at[pl.ds(chunk * step_rows, step_rows), :] if step == 0 else place(block, chunk)
        )
        return pltpu.make_async_remote_copy(
            src_ref=source,
            dst_ref=place(block, chunk),
            send_sem=sem.at[step, chunk],
            recv_sem=recv_sem.at[block, chunk],
            device_id={"dp": to_dp},
            device_id_type=MESH,
        )

    def each(act):
        for step in range(groups):
            for chunk in range(CHUNKS):
                upper, lower = my_dp + step, my_dp - step
                pl.when(upper < groups)(functools.partial(act, upper, chunk, step, left_sem, my_dp - 1, has_left))
                pl.when(lower >= 0)(functools.partial(act, lower, chunk, step, right_sem, my_dp + 1, has_right))

    def start(block, chunk, step, sem, to_dp, sends):
        if step > 0:
            copy(block, chunk, step, sem, my_dp).wait_recv()

        @pl.when(sends)
        def _():
            copy(block, chunk, step, sem, to_dp).start()

    def drain(block, chunk, step, sem, to_dp, sends):
        @pl.when(sends)
        def _():
            copy(block, chunk, step, sem, to_dp).wait_send()

    each(start)
    each(drain)
    own.wait()


def gather(block, groups):
    rows, columns = block.shape
    return pl.pallas_call(
        functools.partial(gather_kernel, groups),
        out_shape=jax.ShapeDtypeStruct((rows, columns * groups), block.dtype),
        in_specs=[pl.BlockSpec(memory_space=pl.ANY)],
        out_specs=pl.BlockSpec(memory_space=pl.ANY),
        scratch_shapes=[
            pltpu.SemaphoreType.DMA((groups, CHUNKS)),
            pltpu.SemaphoreType.DMA((groups, CHUNKS)),
            pltpu.SemaphoreType.DMA((groups, CHUNKS)),
            pltpu.SemaphoreType.DMA,
        ],
        compiler_params=pltpu.CompilerParams(collective_id=1, has_side_effects=True),
        name="gather",
    )(block)


def body(token_ids, token_count, out_grads, master_rows, first_moment, second_moment):
    owners = lax.axis_size("vocab")
    groups = lax.axis_size("dp")
    rows_own, columns = master_rows.shape
    tok_slots = token_ids.shape[0]
    first_new = VOCAB - rows_own * owners
    position = jnp.arange(tok_slots)
    is_live = (position < token_count[0]) & (token_ids >= first_new)
    new_index = token_ids - first_new
    owner_of = jnp.where(is_live, new_index // rows_own, -1)
    row_in_owner = new_index % rows_own
    earlier = (owner_of[:, None] == owner_of[None, :]) & (position[:, None] < position[None, :])
    my_rank = jnp.sum(earlier.astype(jnp.int32), axis=0)
    slot_index = jnp.where(is_live, owner_of * CAP + my_rank, -1)
    placing = jnp.arange(owners * CAP)[:, None] == slot_index[None, :]
    outgoing = jnp.dot(
        placing.astype(jnp.bfloat16), out_grads, preferred_element_type=jnp.float32
    ).astype(jnp.bfloat16)
    slot_row = jnp.max(jnp.where(placing, row_in_owner[None, :], -1), axis=1)
    upper_part = jnp.where(slot_row >= 0, slot_row // 16, -1)
    lower_part = jnp.where(slot_row >= 0, slot_row % 16, 0)
    lane = jnp.arange(LANES)[None, :]
    row_pairs = jnp.where(lane == 0, upper_part[:, None], jnp.where(lane == 1, lower_part[:, None], 0))
    row_pairs = row_pairs.astype(jnp.bfloat16).reshape(1, owners, CAP, LANES)
    outgoing = outgoing.reshape(owners, CAP, groups, columns).transpose(2, 0, 1, 3)
    outgoing = jnp.concatenate(
        [outgoing, jnp.broadcast_to(row_pairs, (groups, owners, CAP, LANES))], axis=3
    )
    arrived = exchange(outgoing).reshape(-1, columns + LANES)
    pairs = arrived[:, columns : columns + 2].astype(jnp.float32)
    decoded = pairs[:, 0] * 16.0 + pairs[:, 1]
    selector = decoded[None, :] == jnp.arange(rows_own, dtype=jnp.float32)[:, None]
    gradient = jnp.dot(
        selector.astype(jnp.bfloat16), arrived[:, :columns], preferred_element_type=jnp.float32
    )
    new_first = beta_one * first_moment + (1.0 - beta_one) * gradient
    new_second = beta_two * second_moment + (1.0 - beta_two) * gradient * gradient
    update = new_first / corr_one / (jnp.sqrt(new_second / corr_two) + epsilon)
    new_master = master_rows - learn_rate * update
    table_rows = gather(new_master.astype(jnp.bfloat16), groups)
    return (new_master, new_first, new_second, table_rows)


def solution(mesh):
    return jax.shard_map(
        body,
        mesh=mesh,
        in_specs=(
            P(("dp", "vocab")),
            P(("dp", "vocab")),
            P(("dp", "vocab"), None),
            P("vocab", "dp"),
            P("vocab", "dp"),
            P("vocab", "dp"),
        ),
        out_specs=(P("vocab", "dp"), P("vocab", "dp"), P("vocab", "dp"), P("vocab", None)),
        check_vma=False,
    )
```

time: 185 us -> 136 us (0.74)
  waiting for transfers between devices: 129 us -> 0 us
  Pallas kernels: 0 us -> 113 us
  starting transfers between devices: 17.1 us -> 0 us
  between operations: 14.9 us -> 1.51 us
  local copies, waits for them, and re-layouts: 11 us -> 8.13 us
    pallas_call x0 -> x2, Pallas kernels: none -> 113 us  [the longest x1 91.2 us: gather(): pl.pallas_call(functools.partial(gather_kernel, groups), out_shape=jax.Sh...]
    all_gather x1 -> x0, waiting for transfers between devices: 95.4 us -> none  [body(): lax.all_gather(new_master.astype(jnp.bfloat16), 'dp', axis=1, tiled=True)]
    all_to_all x4 -> x0, waiting for transfers between devices: 33.6 us -> none  [the longest x1 15.4 us: body(): lax.all_to_all(outgoing, 'dp', split_axis=1, concat_axis=0, tiled=True)]
    all_to_all x4 -> x0, starting transfers between devices: 17.1 us -> none  [the longest x1 6.35 us: body(): lax.all_to_all(tiled_pairs, 'dp', split_axis=1, concat_axis=0, tiled=True)]
    all_to_all x6 -> x0, local copies, waits for them, and re-layouts: 3.17 us -> none  [the longest x2 2.22 us: body(): lax.all_to_all(outgoing, 'dp', split_axis=1, concat_axis=0, tiled=True)]
    reshape x0 -> x2, local copies, waits for them, and re-layouts: none -> 1.92 us  [body(): outgoing.reshape(owners, CAP, groups, columns).transpose(2, 0, 1, 3)]
    unnamed x5 -> x4, local copies, waits for them, and re-layouts: 6.81 us -> 5.28 us
  transfers between devices with their start and end apart: 5 -> 0, of which waited for: 5 -> 0; matrix products, arithmetic and copies ran while one was open for 2% -> 0% of each run, Pallas kernels for 0% -> 0%
where the time goes in v1:
time: 136 us
  Pallas kernels  113 us (83%)
  matrix products  10.6 us (8%)
  local copies, waits for them, and re-layouts  8.13 us (6%)
  other arithmetic  2.66 us (2%)
  between operations  1.51 us (1%)
    pallas_call x1, Pallas kernels, gather(): pl.pallas_call(functools.partial(gather_kernel, groups), out_shape=jax.Sh...  91.2 us
    pallas_call x1, Pallas kernels, exchange(): pl.pallas_call(functools.partial(exchange_kernel, groups, owners), out_sh...  21.7 us
    dot_general x1, matrix products, body(): jnp.dot(selector.astype(jnp.bfloat16), arrived[:, :columns], preferred_el...  9.17 us
    unnamed x4, local copies, waits for them, and re-layouts  5.28 us

profile of v1, /device:TPU:0, one launch (start us, length us, event | category | flops | bytes accessed | tf_op | source)
XLA Modules:
  0.0 135.8 jit_solution(8989400398188638718)
XLA Ops:
  0.6 0.0 copy-start
  1.4 0.7 fusion.10
  2.1 0.1 convert_reduce_fusion
  2.3 0.7 add_select_fusion.2
  2.9 0.1 select_reduce_fusion
  3.1 0.1 reduce_max.12
  3.2 0.1 select_convert_fusion
  3.3 0.0 copy-done
  3.3 1.4 %convolution_convert_fusion = bf16[64,5120]{1,0:T(8,128)(2,1)} fusion(bf16[256,5120]{1,0:T(8,128)(2,1)S(1)} %copy-done, s32[256]{0:T(256)S(1)} %get-tuple-element.10), kind=kOutput, calls=%fused_computation | convolution fusion | flops 168116224 | bytes 3277824 | tf_op jit(solution)/shard_map/dot_general | solution.py:194
  4.7 1.9 %reshape.104 = bf16[8,8,4,1280]{3,2,1,0:T(4,128)(2,1)S(1)} reshape(bf16[64,5120]{1,0:T(8,128)(2,1)} %convolution_convert_fusion) | data formatting | bytes 1310720 | tf_op jit(solution)/shard_map/reshape | solution.py:203
  6.6 0.1 copy.16
  6.6 0.9 pad_maximum_fusion.out_ref
  7.6 21.7 %exchange.1 = bf16[32,8,1408]{2,1,0:T(8,128)(2,1)} custom-call(bf16[4,8,8,1408]{3,2,1,0:T(8,128)(2,1)} %pad_maximum_fusion.out_ref), custom_call_target="tpu_custom_call" | custom-call | tf_op jit(solution)/shard_map/exchange/pallas_call | solution.py:82
  29.2 0.8 slice.16
  30.1 0.1 copy.14
  30.2 9.2 %fusion.11 = (bf16[512,1280]{1,0:T(8,128)(2,1)}, f32[512,1280]{1,0:T(8,128)}, f32[512,1280]{1,0:T(8,128)}, f32[512,1280]{1,0:T(8,128)}) fusion(f32[512,1280]{1,0:T(8,128)} %param.9, f32[512,1280]{1,0:T(8,128)} %param.10, f32[512,1280]{1,0:T(8,128)} %param.11, bf16[256,1408]{1,0:T(8,128)(2,1)} %bitcast.11, f32[256]{0:T(256)S(1)} %bitcast.12), kind=kOutput, calls=%fused_computation.43 | convolution fusion | flops 344850432 | bytes 17695744 | tf_op jit(solution)/shard_map/dot_general | solution.py:211
  39.4 91.2 %gather.1 = bf16[512,5120]{1,0:T(8,128)(2,1)} custom-call(bf16[512,1280]{1,0:T(8,128)(2,1)} %get-tuple-element.4.block_ref), custom_call_target="tpu_custom_call" | custom-call | tf_op jit(solution)/shard_map/gather/pallas_call | solution.py:163
  130.6 5.2 %copy.19 = bf16[512,5120]{1,0:T(8,128)(2,1)} copy(bf16[512,5120]{1,0:T(8,128)(2,1)} %gather.1) | data formatting | bytes 10485760
  (5 shorter events, 0.0 us)
Async XLA Ops:
  0.6 2.7 %copy-start = (bf16[256,5120]{1,0:T(8,128)(2,1)S(1)}, bf16[256,5120]{1,0:T(8,128)(2,1)}, u32[]{:S(2)}) copy-start(bf16[256,5120]{1,0:T(8,128)(2,1)} %param.8) | copy-start | bytes 7864324

commit v2 on v1

v2 whole, which is shorter than its diff:
```python
import functools

import jax
import jax.numpy as jnp
from jax import lax
from jax.experimental import pallas as pl
from jax.experimental.pallas import tpu as pltpu
from jax.sharding import PartitionSpec as P

VOCAB = 152064
CAP = 8
LANES = 128
CHUNKS = 8
KEPT = 4
MESH = pl.DeviceIdType.MESH


beta_one = 0.9
beta_two = 0.999
corr_one = 1.0 - 0.9**10
corr_two = 1.0 - 0.999**10
learn_rate = 0.01
epsilon = 1e-08


def adam(gradient, master, first, second):
    new_first = beta_one * first + (1.0 - beta_one) * gradient
    new_second = beta_two * second + (1.0 - beta_two) * gradient * gradient
    update = new_first / corr_one / (jnp.sqrt(new_second / corr_two) + epsilon)
    return master - learn_rate * update, new_first, new_second


def step_kernel(
    groups,
    owners,
    kept,
    out_ref,
    master_hbm,
    first_hbm,
    second_hbm,
    table_ref,
    arr_ref,
    master_ref,
    first_ref,
    second_ref,
    block_ref,
    send_sem,
    arrive_sem,
    left_sem,
    right_sem,
    recv_sem,
    own_sem,
    load_sem,
):
    my_dp, my_vocab = lax.axis_index("dp"), lax.axis_index("vocab")
    total = groups * owners
    me = my_dp * owners + my_vocab
    rows, columns = master_ref.shape
    step_rows = rows // CHUNKS
    barrier = pltpu.get_barrier_semaphore()
    has_left, has_right = my_dp > 0, my_dp < groups - 1

    loads = [
        pltpu.make_async_copy(src, dst, load_sem.at[i])
        for i, (src, dst) in enumerate(
            ((master_hbm, master_ref), (first_hbm, first_ref), (second_hbm, second_ref))
        )
    ]
    for load in loads:
        load.start()

    def greet(k, carry):
        other = lax.rem(me + k, total)
        pl.semaphore_signal(
            barrier, inc=1, device_id=(other // owners, lax.rem(other, owners)), device_id_type=MESH
        )
        return carry

    lax.fori_loop(1, total, greet, 0)
    own = pltpu.make_async_copy(out_ref.at[my_dp, my_vocab], arr_ref.at[me], own_sem.at[0])
    own.start()
    pl.semaphore_wait(barrier, total - 1)

    def send_copy(k):
        to_dp = lax.rem(k // owners + 1, groups)
        to_vocab = lax.rem(my_vocab + lax.rem(k, owners), owners)
        here = (to_dp == my_dp) & (to_vocab == my_vocab)
        return here, pltpu.make_async_remote_copy(
            src_ref=out_ref.at[to_dp, to_vocab],
            dst_ref=arr_ref.at[me],
            send_sem=send_sem.at[k],
            recv_sem=arrive_sem.at[me],
            device_id=(to_dp, to_vocab),
            device_id_type=MESH,
        )

    def send(k, carry):
        here, copy = send_copy(k)

        @pl.when(jnp.logical_not(here))
        def _():
            copy.start()

        return carry

    lax.fori_loop(0, total, send, 0)

    def arrive(k, carry):
        sender = lax.rem(me + k, total)
        pltpu.make_async_remote_copy(
            src_ref=out_ref.at[my_dp, my_vocab],
            dst_ref=arr_ref.at[sender],
            send_sem=send_sem.at[k],
            recv_sem=arrive_sem.at[sender],
            device_id=(sender // owners, lax.rem(sender, owners)),
            device_id_type=MESH,
        ).wait_recv()
        return carry

    for load in loads:
        load.wait()
    own.wait()
    lax.fori_loop(1, total, arrive, 0)

    tokens = total * arr_ref.shape[1]
    pairs = arr_ref[:, :, columns:].astype(jnp.float32).reshape(tokens, LANES)
    decoded = jnp.broadcast_to(pairs[:, 0:1] * 16.0 + pairs[:, 1:2], (tokens, LANES)).T[0:1, :]
    grads = arr_ref[:, :, :columns].astype(jnp.float32).reshape(tokens, columns).astype(jnp.bfloat16)

    def place(block, chunk):
        start = pl.multiple_of(block * columns, LANES)
        return table_ref.at[pl.ds(chunk * step_rows, step_rows), pl.ds(start, columns)]

    def copy(block, chunk, step, sem, to_dp):
        source = (
            block_ref.at[pl.ds(chunk * step_rows, step_rows), :] if step == 0 else place(block, chunk)
        )
        return pltpu.make_async_remote_copy(
            src_ref=source,
            dst_ref=place(block, chunk),
            send_sem=sem.at[step, chunk],
            recv_sem=recv_sem.at[block, chunk],
            device_id={"dp": to_dp},
            device_id_type=MESH,
        )

    def both(act, step, chunk):
        upper, lower = my_dp + step, my_dp - step
        pl.when(upper < groups)(functools.partial(act, upper, chunk, step, left_sem, my_dp - 1, has_left))
        pl.when(lower >= 0)(functools.partial(act, lower, chunk, step, right_sem, my_dp + 1, has_right))

    def held_back(step, chunk):
        return step >= groups - 1 and chunk >= kept

    def start(block, chunk, step, sem, to_dp, sends):
        if step > 0:
            copy(block, chunk, step, sem, my_dp).wait_recv()
        if not held_back(step + 1, chunk):

            @pl.when(sends)
            def _():
                copy(block, chunk, step, sem, to_dp).start()

    def drain(block, chunk, step, sem, to_dp, sends):
        if not held_back(step + 1, chunk):

            @pl.when(sends)
            def _():
                copy(block, chunk, step, sem, to_dp).wait_send()

    row_iota = lax.broadcasted_iota(jnp.int32, (step_rows, tokens), 0)
    for chunk in range(CHUNKS):
        here = pl.ds(chunk * step_rows, step_rows)
        selector = decoded == (row_iota + chunk * step_rows).astype(jnp.float32)
        gradient = jnp.dot(
            selector.astype(jnp.float32).astype(jnp.bfloat16), grads, preferred_element_type=jnp.float32
        )
        master = adam(gradient, master_ref[here, :], first_ref[here, :], second_ref[here, :])[0]
        block_ref[here, :] = master.astype(jnp.bfloat16)
        if chunk > 0:
            both(start, 0, chunk - 1)
    both(start, 0, CHUNKS - 1)
    own_block = pltpu.make_async_copy(
        block_ref,
        table_ref.at[:, pl.ds(pl.multiple_of(my_dp * columns, LANES), columns)],
        own_sem.at[1],
    )
    own_block.start()
    for step in range(1, groups):
        for chunk in range(CHUNKS):
            if not held_back(step, chunk):
                both(start, step, chunk)
    for step in range(groups):
        for chunk in range(CHUNKS):
            if not held_back(step, chunk):
                both(drain, step, chunk)

    def sent(k, carry):
        here, copy = send_copy(k)

        @pl.when(jnp.logical_not(here))
        def _():
            copy.wait_send()

        return carry

    lax.fori_loop(0, total, sent, 0)
    own_block.wait()


def exchange_and_gather(outgoing, master, first, second, kept):
    groups, owners, cap, width = outgoing.shape
    total = groups * owners
    rows, columns = master.shape
    return pl.pallas_call(
        functools.partial(step_kernel, groups, owners, kept),
        out_shape=(
            jax.ShapeDtypeStruct((rows, columns * groups), jnp.bfloat16),
            jax.ShapeDtypeStruct((total, cap, width), outgoing.dtype),
        ),
        in_specs=[pl.BlockSpec(memory_space=pltpu.VMEM)] + [pl.BlockSpec(memory_space=pl.ANY)] * 3,
        out_specs=(pl.BlockSpec(memory_space=pl.ANY), pl.BlockSpec(memory_space=pltpu.VMEM)),
        scratch_shapes=[
            pltpu.VMEM((rows, columns), jnp.float32),
            pltpu.VMEM((rows, columns), jnp.float32),
            pltpu.VMEM((rows, columns), jnp.float32),
            pltpu.VMEM((rows, columns), jnp.bfloat16),
            pltpu.SemaphoreType.DMA((total,)),
            pltpu.SemaphoreType.DMA((total,)),
            pltpu.SemaphoreType.DMA((groups, CHUNKS)),
            pltpu.SemaphoreType.DMA((groups, CHUNKS)),
            pltpu.SemaphoreType.DMA((groups, CHUNKS)),
            pltpu.SemaphoreType.DMA((2,)),
            pltpu.SemaphoreType.DMA((3,)),
        ],
        compiler_params=pltpu.CompilerParams(collective_id=0, has_side_effects=True),
        name="exchange_and_gather",
    )(outgoing, master, first, second)


def copy_kernel(src_ref, dst_ref):
    dst_ref[...] = src_ref[...]


def fresh_copy(table):
    rows, width = table.shape
    block = pl.BlockSpec((rows // CHUNKS, width), lambda i: (i, 0))
    return pl.pallas_call(
        copy_kernel,
        out_shape=jax.ShapeDtypeStruct(table.shape, table.dtype),
        grid=(CHUNKS,),
        in_specs=[block],
        out_specs=block,
        cost_estimate=pl.CostEstimate(flops=0, bytes_accessed=4 * rows * width, transcendentals=0),
        name="fresh_copy",
    )(table)


def patch_kernel(groups, tail_ref, old_ref, table_ref, sem):
    my_dp = lax.axis_index("dp")
    rows, columns = tail_ref.shape
    top = table_ref.shape[0] - rows
    far = pl.multiple_of(jnp.where(my_dp == 0, groups - 1, 0) * columns, LANES)

    @pl.when((my_dp == 0) | (my_dp == groups - 1))
    def _():
        copy = pltpu.make_async_copy(tail_ref, table_ref.at[pl.ds(top, rows), pl.ds(far, columns)], sem)
        copy.start()
        copy.wait()


def patch(tail, table, groups):
    return pl.pallas_call(
        functools.partial(patch_kernel, groups),
        out_shape=jax.ShapeDtypeStruct(table.shape, table.dtype),
        in_specs=[pl.BlockSpec(memory_space=pltpu.VMEM), pl.BlockSpec(memory_space=pl.ANY)],
        out_specs=pl.BlockSpec(memory_space=pl.ANY),
        scratch_shapes=[pltpu.SemaphoreType.DMA],
        input_output_aliases={1: 0},
        name="patch",
    )(tail, table)


def body(token_ids, token_count, out_grads, master_rows, first_moment, second_moment):
    owners = lax.axis_size("vocab")
    groups = lax.axis_size("dp")
    rows_own, columns = master_rows.shape
    tok_slots = token_ids.shape[0]
    first_new = VOCAB - rows_own * owners
    position = jnp.arange(tok_slots)
    is_live = (position < token_count[0]) & (token_ids >= first_new)
    new_index = token_ids - first_new
    owner_of = jnp.where(is_live, new_index // rows_own, -1)
    row_in_owner = new_index % rows_own
    earlier = (owner_of[:, None] == owner_of[None, :]) & (position[:, None] < position[None, :])
    my_rank = jnp.sum(earlier.astype(jnp.int32), axis=0)
    slot_index = jnp.where(is_live, owner_of * CAP + my_rank, -1)
    placing = jnp.arange(owners * CAP)[:, None] == slot_index[None, :]
    outgoing = jnp.dot(
        placing.astype(jnp.bfloat16), out_grads, preferred_element_type=jnp.float32
    ).astype(jnp.bfloat16)
    slot_row = jnp.max(jnp.where(placing, row_in_owner[None, :], -1), axis=1)
    upper_part = jnp.where(slot_row >= 0, slot_row // 16, -1)
    lower_part = jnp.where(slot_row >= 0, slot_row % 16, 0)
    lane = jnp.arange(LANES)[None, :]
    row_pairs = jnp.where(lane == 0, upper_part[:, None], jnp.where(lane == 1, lower_part[:, None], 0))
    row_pairs = row_pairs.astype(jnp.bfloat16).reshape(1, owners, CAP, LANES)
    outgoing = outgoing.reshape(owners, CAP, groups, columns).transpose(2, 0, 1, 3)
    outgoing = jnp.concatenate(
        [outgoing, jnp.broadcast_to(row_pairs, (groups, owners, CAP, LANES))], axis=3
    )
    kept = KEPT if groups >= 4 else CHUNKS
    table, arrived = exchange_and_gather(outgoing, master_rows, first_moment, second_moment, kept)
    if kept < CHUNKS:
        my_dp = lax.axis_index("dp")
        top = rows_own // CHUNKS * kept
        sent = jnp.where(my_dp == 1, groups - 1, 0) * columns
        tail = lax.dynamic_slice(table, (top, sent), (rows_own - top, columns))
        tail = lax.ppermute(tail, "dp", [(1, 0), (groups - 2, groups - 1)])
        table = fresh_copy(table)
    arrived = arrived.reshape(-1, columns + LANES)
    pairs = arrived[:, columns : columns + 2].astype(jnp.float32)
    decoded = pairs[:, 0] * 16.0 + pairs[:, 1]
    selector = decoded[None, :] == jnp.arange(rows_own, dtype=jnp.float32)[:, None]
    gradient = jnp.dot(
        selector.astype(jnp.bfloat16), arrived[:, :columns], preferred_element_type=jnp.float32
    )
    new_master, new_first, new_second = adam(gradient, master_rows, first_moment, second_moment)
    if kept < CHUNKS:
        table = patch(tail, table, groups)
    return (new_master, new_first, new_second, table)


def solution(mesh):
    return jax.shard_map(
        body,
        mesh=mesh,
        in_specs=(
            P(("dp", "vocab")),
            P(("dp", "vocab")),
            P(("dp", "vocab"), None),
            P("vocab", "dp"),
            P("vocab", "dp"),
            P("vocab", "dp"),
        ),
        out_specs=(P("vocab", "dp"), P("vocab", "dp"), P("vocab", "dp"), P("vocab", None)),
        check_vma=False,
    )
```

time: 136 us -> 128 us (0.941)
  Pallas kernels: 113 us -> 107 us
  local copies, waits for them, and re-layouts: 8.13 us -> 4.63 us
    pallas_call x2 -> x3, Pallas kernels: 113 us -> 107 us  [the longest x1 98.3 us: exchange_and_gather(): pl.pallas_call(functools.partial(step_kernel, groups, owners, kept), out_...]
    unnamed x4 -> x3, local copies, waits for them, and re-layouts: 5.28 us -> 0.09 us
  transfers between devices with their start and end apart: 0 -> 1, of which waited for: 0 -> 1; matrix products, arithmetic and copies ran while one was open for 0% -> 8% of each run, Pallas kernels for 0% -> 6%
where the time goes in v2:
time: 128 us; the launch traced here: 127 us
  Pallas kernels  107 us (84%)
  matrix products  9.38 us (7%)
  local copies, waits for them, and re-layouts  4.63 us (4%)
  other arithmetic  2.66 us (2%)
  between operations  1.53 us (1%)
  starting transfers between devices  1.29 us (1%)
    pallas_call x1, Pallas kernels, exchange_and_gather(): pl.pallas_call(functools.partial(step_kernel, groups, owners, kept), out_...  98.3 us
    dot_general x1, matrix products, body(): jnp.dot(selector.astype(jnp.bfloat16), arrived[:, :columns], preferred_el...  8.81 us
    pallas_call x1, Pallas kernels, fresh_copy(): pl.pallas_call(copy_kernel, out_shape=jax.ShapeDtypeStruct(table.shape, t...  7.23 us
  transfers between devices with their start and end apart: 1, of which 1 were waited for; matrix products, arithmetic and copies ran while one was open for 8% of the time, Pallas kernels for 6%

profile of v2, /device:TPU:0, one launch (start us, length us, event | category | flops | bytes accessed | tf_op | source)
XLA Modules:
  0.0 127.4 jit_solution(10785723447323668617)
XLA Ops:
  0.6 0.0 copy-start
  1.5 0.7 fusion.10
  2.2 0.1 convert_reduce_fusion
  2.3 0.7 add_select_fusion.2
  3.0 0.1 select_reduce_fusion
  3.1 0.1 reduce_max.12
  3.2 0.0 copy-done
  3.2 0.6 convolution_convert_fusion
  3.8 1.3 %reshape.104 = bf16[8,8,4,1280]{3,2,1,0:T(4,128)(2,1)} reshape(bf16[64,5120]{1,0:T(8,128)(2,1)S(1)} %convolution_convert_fusion) | data formatting | bytes 1310720 | tf_op jit(solution)/shard_map/reshape | solution.py:308
  5.1 1.2 copy.17
  6.2 0.1 select_convert_fusion
  6.4 0.9 pad_maximum_fusion.out_ref
  7.3 98.3 %exchange_and_gather.1 = (bf16[512,5120]{1,0:T(8,128)(2,1)}, bf16[32,8,1408]{2,1,0:T(8,128)(2,1)}) custom-call(bf16[4,8,8,1408]{3,2,1,0:T(8,128)(2,1)} %pad_maximum_fusion.out_ref, f32[512,1280]{1,0:T(8,128)} %master_hbm.1, f32[512,1280]{1,0:T(8,128)} %first_hbm.1, f32[512,1280]{1,0:T(8,128)} %second_hbm.1), custom_call_target="tpu_custom_call" | custom-call | tf_op jit(solution)/shard_map/exchange_and_gather/pallas_call | solution.py:215
  105.6 1.1 constant_dynamic-slice_fusion
  106.8 1.3 %collective-permute-start = (bf16[256,1280]{1,0:T(8,128)(2,1)S(1)}, bf16[256,1280]{1,0:T(8,128)(2,1)}, u32[]{:S(2)}, u32[]{:S(2)}) collective-permute-start(bf16[256,1280]{1,0:T(8,128)(2,1)S(1)} %constant_dynamic-slice_fusion), channel_id=1, source_target_pairs={{8,0},{16,24},{9,1},{17,25},{10,2},{18,26},{11,3},{19,27},{12,4},{... | collective-permute-start | bytes 1966088 | tf_op jit(solution)/shard_map/ppermute | solution.py:319
  108.1 7.2 %fresh_copy.1.old_ref = bf16[512,5120]{1,0:T(8,128)(2,1)} custom-call(bf16[512,5120]{1,0:T(8,128)(2,1)} %get-tuple-element.7.src_ref), custom_call_target="tpu_custom_call" | custom-call | bytes 10485760 | tf_op jit(solution)/shard_map/fresh_copy/pallas_call | solution.py:248
  115.3 0.8 slice.16
  116.1 0.1 copy.15
  116.2 8.8 %multiply_subtract_fusion = (f32[512,1280]{1,0:T(8,128)}, f32[512,1280]{1,0:T(8,128)}, f32[512,1280]{1,0:T(8,128)}) fusion(f32[512,1280]{1,0:T(8,128)} %master_hbm.1, f32[512,1280]{1,0:T(8,128)} %first_hbm.1, f32[512,1280]{1,0:T(8,128)} %second_hbm.1, bf16[256,1408]{1,0:T(8,128)(2,1)} %bitcast.11, f32[256]{0:T(256)S(1)} %bitcast.12), kind=kOutput, calls=%fused_computation.3 | convolution fusion | flops 344195072 | bytes 16385024 | tf_op jit(solution)/shard_map/dot_general | solution.py:325
  125.0 0.5 collective-permute-done.tail_ref
  125.5 1.9 %patch.1 = bf16[512,5120]{1,0:T(8,128)(2,1)} custom-call(bf16[256,1280]{1,0:T(8,128)(2,1)} %collective-permute-done.tail_ref, bf16[512,5120]{1,0:T(8,128)(2,1)} %fresh_copy.1.old_ref), custom_call_target="tpu_custom_call", output_to_operand_aliasing={{}: (1, {})} | custom-call | tf_op jit(solution)/shard_map/patch/pallas_call | solution.py:273
  (5 shorter events, 0.0 us)
Async XLA Ops:
  0.6 2.6 %copy-start = (bf16[256,5120]{1,0:T(8,128)(2,1)S(1)}, bf16[256,5120]{1,0:T(8,128)(2,1)}, u32[]{:S(2)}) copy-start(bf16[256,5120]{1,0:T(8,128)(2,1)} %param.8) | copy-start | bytes 7864324
  106.8 18.8 %collective-permute-start = (bf16[256,1280]{1,0:T(8,128)(2,1)S(1)}, bf16[256,1280]{1,0:T(8,128)(2,1)}, u32[]{:S(2)}, u32[]{:S(2)}) collective-permute-start(bf16[256,1280]{1,0:T(8,128)(2,1)S(1)} %constant_dynamic-slice_fusion), channel_id=1, source_target_pairs={{8,0},{16,24},{9,1},{17,25},{10,2},{18,26},{11,3},{19,27},{12,4},{... | collective-permute-start | bytes 1966088 | tf_op jit(solution)/shard_map/ppermute | solution.py:319

commit v3 on v2

--- a/solution.py
+++ b/solution.py
@@ -11,7 +11,7 @@
 CAP = 8
 LANES = 128
 CHUNKS = 8
-KEPT = 4
+KEPT = 8
 MESH = pl.DeviceIdType.MESH
 
 
@@ -35,17 +35,21 @@
     owners,
     kept,
     out_ref,
+    ids_ref,
     master_hbm,
     first_hbm,
     second_hbm,
     table_ref,
-    arr_ref,
     master_ref,
     first_ref,
     second_ref,
+    arr_ref,
+    tag_ref,
     block_ref,
     send_sem,
     arrive_sem,
+    tag_send_sem,
+    tag_sem,
     left_sem,
     right_sem,
     recv_sem,
@@ -77,29 +81,49 @@
         return carry
 
     lax.fori_loop(1, total, greet, 0)
-    own = pltpu.make_async_copy(out_ref.at[my_dp, my_vocab], arr_ref.at[me], own_sem.at[0])
+    def part(to_dp, to_vocab):
+        row = pl.multiple_of(to_vocab * CAP, CAP)
+        return out_ref.at[pl.ds(row, CAP), pl.ds(pl.multiple_of(to_dp * columns, LANES), columns)]
+
+    own = pltpu.make_async_copy(part(my_dp, my_vocab), arr_ref.at[me], own_sem.at[0])
     own.start()
+    own_tag = pltpu.make_async_copy(ids_ref.at[my_vocab], tag_ref.at[me], own_sem.at[2])
+    own_tag.start()
     pl.semaphore_wait(barrier, total - 1)
 
-    def send_copy(k):
+    def pair(k, slot, to_dp, to_vocab):
+        return (
+            pltpu.make_async_remote_copy(
+                src_ref=ids_ref.at[to_vocab],
+                dst_ref=tag_ref.at[slot],
+                send_sem=tag_send_sem.at[k],
+                recv_sem=tag_sem.at[slot],
+                device_id=(to_dp, to_vocab),
+                device_id_type=MESH,
+            ),
+            pltpu.make_async_remote_copy(
+                src_ref=part(to_dp, to_vocab),
+                dst_ref=arr_ref.at[slot],
+                send_sem=send_sem.at[k],
+                recv_sem=arrive_sem.at[slot],
+                device_id=(to_dp, to_vocab),
+                device_id_type=MESH,
+            ),
+        )
+
+    def send_pair(k):
         to_dp = lax.rem(k // owners + 1, groups)
         to_vocab = lax.rem(my_vocab + lax.rem(k, owners), owners)
         here = (to_dp == my_dp) & (to_vocab == my_vocab)
-        return here, pltpu.make_async_remote_copy(
-            src_ref=out_ref.at[to_dp, to_vocab],
-            dst_ref=arr_ref.at[me],
-            send_sem=send_sem.at[k],
-            recv_sem=arrive_sem.at[me],
-            device_id=(to_dp, to_vocab),
-            device_id_type=MESH,
-        )
+        return here, pair(k, me, to_dp, to_vocab)
 
     def send(k, carry):
-        here, copy = send_copy(k)
+        here, copies = send_pair(k)
 
         @pl.when(jnp.logical_not(here))
         def _():
-            copy.start()
+            copies[0].start()
+            copies[1].start()
 
         return carry
 
@@ -107,25 +131,21 @@
 
     def arrive(k, carry):
         sender = lax.rem(me + k, total)
-        pltpu.make_async_remote_copy(
-            src_ref=out_ref.at[my_dp, my_vocab],
-            dst_ref=arr_ref.at[sender],
-            send_sem=send_sem.at[k],
-            recv_sem=arrive_sem.at[sender],
-            device_id=(sender // owners, lax.rem(sender, owners)),
-            device_id_type=MESH,
-        ).wait_recv()
+        tag, grads = pair(k, sender, sender // owners, lax.rem(sender, owners))
+        tag.wait_recv()
+        grads.wait_recv()
         return carry
 
     for load in loads:
         load.wait()
     own.wait()
+    own_tag.wait()
     lax.fori_loop(1, total, arrive, 0)
 
-    tokens = total * arr_ref.shape[1]
-    pairs = arr_ref[:, :, columns:].astype(jnp.float32).reshape(tokens, LANES)
+    tokens = total * CAP
+    pairs = tag_ref[...].astype(jnp.float32).reshape(tokens, LANES)
     decoded = jnp.broadcast_to(pairs[:, 0:1] * 16.0 + pairs[:, 1:2], (tokens, LANES)).T[0:1, :]
-    grads = arr_ref[:, :, :columns].astype(jnp.float32).reshape(tokens, columns).astype(jnp.bfloat16)
+    grads = arr_ref[...].astype(jnp.float32).reshape(tokens, columns).astype(jnp.bfloat16)
 
     def place(block, chunk):
         start = pl.multiple_of(block * columns, LANES)
@@ -175,8 +195,11 @@
         gradient = jnp.dot(
             selector.astype(jnp.float32).astype(jnp.bfloat16), grads, preferred_element_type=jnp.float32
         )
-        master = adam(gradient, master_ref[here, :], first_ref[here, :], second_ref[here, :])[0]
+        master, first, second = adam(gradient, master_ref[here, :], first_ref[here, :], second_ref[here, :])
         block_ref[here, :] = master.astype(jnp.bfloat16)
+        master_ref[here, :] = master
+        first_ref[here, :] = first
+        second_ref[here, :] = second
         if chunk > 0:
             both(start, 0, chunk - 1)
     both(start, 0, CHUNKS - 1)
@@ -196,11 +219,12 @@
                 both(drain, step, chunk)
 
     def sent(k, carry):
-        here, copy = send_copy(k)
+        here, copies = send_pair(k)
 
         @pl.when(jnp.logical_not(here))
         def _():
-            copy.wait_send()
+            copies[0].wait_send()
+            copies[1].wait_send()
 
         return carry
 
@@ -208,34 +232,41 @@
     own_block.wait()
 
 
-def exchange_and_gather(outgoing, master, first, second, kept):
-    groups, owners, cap, width = outgoing.shape
+def exchange_and_gather(outgoing, ids, master, first, second, groups, kept):
+    owners = ids.shape[0]
     total = groups * owners
     rows, columns = master.shape
+    anywhere = pl.BlockSpec(memory_space=pl.ANY)
+    held = pl.BlockSpec(memory_space=pltpu.VMEM)
     return pl.pallas_call(
         functools.partial(step_kernel, groups, owners, kept),
         out_shape=(
-            jax.ShapeDtypeStruct((rows, columns * groups), jnp.bfloat16),
-            jax.ShapeDtypeStruct((total, cap, width), outgoing.dtype),
-        ),
-        in_specs=[pl.BlockSpec(memory_space=pltpu.VMEM)] + [pl.BlockSpec(memory_space=pl.ANY)] * 3,
-        out_specs=(pl.BlockSpec(memory_space=pl.ANY), pl.BlockSpec(memory_space=pltpu.VMEM)),
-        scratch_shapes=[
+            pltpu.VMEM((rows, columns * groups), jnp.bfloat16),
             pltpu.VMEM((rows, columns), jnp.float32),
             pltpu.VMEM((rows, columns), jnp.float32),
             pltpu.VMEM((rows, columns), jnp.float32),
+        ),
+        in_specs=[anywhere] * 2 + [pl.BlockSpec(memory_space=pltpu.HBM)] * 3,
+        out_specs=(held, held, held, held),
+        scratch_shapes=[
+            pltpu.VMEM((total, CAP, columns), jnp.bfloat16),
+            pltpu.VMEM((total, CAP, LANES), jnp.bfloat16),
             pltpu.VMEM((rows, columns), jnp.bfloat16),
+            pltpu.SemaphoreType.DMA((total,)),
+            pltpu.SemaphoreType.DMA((total,)),
             pltpu.SemaphoreType.DMA((total,)),
             pltpu.SemaphoreType.DMA((total,)),
             pltpu.SemaphoreType.DMA((groups, CHUNKS)),
             pltpu.SemaphoreType.DMA((groups, CHUNKS)),
             pltpu.SemaphoreType.DMA((groups, CHUNKS)),
-            pltpu.SemaphoreType.DMA((2,)),
+            pltpu.SemaphoreType.DMA((3,)),
             pltpu.SemaphoreType.DMA((3,)),
         ],
-        compiler_params=pltpu.CompilerParams(collective_id=0, has_side_effects=True),
+        compiler_params=pltpu.CompilerParams(
+            collective_id=0, has_side_effects=True, vmem_limit_bytes=20 * 2**20
+        ),
         name="exchange_and_gather",
-    )(outgoing, master, first, second)
+    )(outgoing, ids, master, first, second)
 
 
 def copy_kernel(src_ref, dst_ref):
@@ -304,30 +335,18 @@
     lower_part = jnp.where(slot_row >= 0, slot_row % 16, 0)
     lane = jnp.arange(LANES)[None, :]
     row_pairs = jnp.where(lane == 0, upper_part[:, None], jnp.where(lane == 1, lower_part[:, None], 0))
-    row_pairs = row_pairs.astype(jnp.bfloat16).reshape(1, owners, CAP, LANES)
-    outgoing = outgoing.reshape(owners, CAP, groups, columns).transpose(2, 0, 1, 3)
-    outgoing = jnp.concatenate(
-        [outgoing, jnp.broadcast_to(row_pairs, (groups, owners, CAP, LANES))], axis=3
+    row_pairs = row_pairs.astype(jnp.bfloat16).reshape(owners, CAP, LANES)
+    kept = KEPT if groups >= 4 else CHUNKS
+    table, new_master, new_first, new_second = exchange_and_gather(
+        outgoing, row_pairs, master_rows, first_moment, second_moment, groups, kept
     )
-    kept = KEPT if groups >= 4 else CHUNKS
-    table, arrived = exchange_and_gather(outgoing, master_rows, first_moment, second_moment, kept)
     if kept < CHUNKS:
         my_dp = lax.axis_index("dp")
         top = rows_own // CHUNKS * kept
         sent = jnp.where(my_dp == 1, groups - 1, 0) * columns
         tail = lax.dynamic_slice(table, (top, sent), (rows_own - top, columns))
         tail = lax.ppermute(tail, "dp", [(1, 0), (groups - 2, groups - 1)])
-        table = fresh_copy(table)
-    arrived = arrived.reshape(-1, columns + LANES)
-    pairs = arrived[:, columns : columns + 2].astype(jnp.float32)
-    decoded = pairs[:, 0] * 16.0 + pairs[:, 1]
-    selector = decoded[None, :] == jnp.arange(rows_own, dtype=jnp.float32)[:, None]
-    gradient = jnp.dot(
-        selector.astype(jnp.bfloat16), arrived[:, :columns], preferred_element_type=jnp.float32
-    )
-    new_master, new_first, new_second = adam(gradient, master_rows, first_moment, second_moment)
-    if kept < CHUNKS:
-        table = patch(tail, table, groups)
+        table = patch(tail, fresh_copy(table), groups)
     return (new_master, new_first, new_second, table)
 
 

time: 128 us -> 127 us (level)
  matrix products: 9.38 us -> 0.57 us
  local copies, waits for them, and re-layouts: 4.63 us -> 11.5 us
  Pallas kernels: 107 us -> 112 us
  starting transfers between devices: 1.29 us -> 0 us
    pallas_call x1, Pallas kernels: 98.3 us -> 112 us  [exchange_and_gather(): pl.pallas_call(functools.partial(step_kernel, groups, owners, kept), out_...]
    unnamed x3 -> x12, local copies, waits for them, and re-layouts: 0.09 us -> 11.4 us
    pallas_call x2 -> x0, Pallas kernels: 9.16 us -> none  [the longest x1 7.23 us: fresh_copy(): pl.pallas_call(copy_kernel, out_shape=jax.ShapeDtypeStruct(table.shape, t...]
    dot_general x1 -> x0, matrix products: 8.81 us -> none  [body(): jnp.dot(selector.astype(jnp.bfloat16), arrived[:, :columns], preferred_el...]
    reshape x2 -> x0, local copies, waits for them, and re-layouts: 2.46 us -> none  [body(): outgoing.reshape(owners, CAP, groups, columns).transpose(2, 0, 1, 3)]
    ppermute x1 -> x0, starting transfers between devices: 1.29 us -> none  [body(): tail = lax.ppermute(tail, 'dp', [(1, 0), (groups - 2, groups - 1)])]
  transfers between devices with their start and end apart: 1 -> 0, of which waited for: 1 -> 0; matrix products, arithmetic and copies ran while one was open for 8% -> 0% of each run, Pallas kernels for 6% -> 0%
where the time goes in v3:
time: 127 us
  Pallas kernels  112 us (88%)
  local copies, waits for them, and re-layouts  11.5 us (9%)
  other arithmetic  1.72 us (1%)
  between operations  1.49 us (1%)
    pallas_call x1, Pallas kernels, exchange_and_gather(): pl.pallas_call(functools.partial(step_kernel, groups, owners, kept), out_...  112 us
    unnamed x12, local copies, waits for them, and re-layouts  11.4 us

profile of v3, /device:TPU:0, one launch (start us, length us, event | category | flops | bytes accessed | tf_op | source)
XLA Modules:
  0.0 126.9 jit_solution(2399470849491527124)
XLA Ops:
  0.6 0.0 copy-start
  1.5 0.7 and_select_fusion
  2.1 0.1 convert_reduce_fusion
  2.3 0.7 add_select_fusion.2
  3.0 0.1 select_reduce_fusion
  3.1 0.1 reduce_max.12
  3.2 0.0 copy-start.1
  3.2 0.1 select_convert_fusion.ids_ref
  3.3 0.0 copy-done
  3.3 0.6 convolution_convert_fusion.out_ref
  3.9 1.0 copy-done.1
  4.9 0.0 copy-start.2
  4.9 1.7 %copy-done.2 = f32[512,1280]{1,0:T(8,128)S(1)} copy-done((f32[512,1280]{1,0:T(8,128)S(1)}, f32[512,1280]{1,0:T(8,128)}, u32[]{:S(2)}) %copy-start.2) | copy-done | bytes 2621464
  6.6 0.0 copy-start.3
  6.6 1.7 %copy-done.3 = f32[512,1280]{1,0:T(8,128)S(1)} copy-done((f32[512,1280]{1,0:T(8,128)S(1)}, f32[512,1280]{1,0:T(8,128)}, u32[]{:S(2)}) %copy-start.3) | copy-done | bytes 2621464
  8.4 111.7 %exchange_and_gather.1 = (bf16[512,5120]{1,0:T(8,128)(2,1)S(1)}, f32[512,1280]{1,0:T(8,128)S(1)}, f32[512,1280]{1,0:T(8,128)S(1)}, f32[512,1280]{1,0:T(8,128)S(1)}) custom-call(bf16[64,5120]{1,0:T(8,128)(2,1)S(1)} %convolution_convert_fusion.out_ref, bf16[8,8,128]{2,1,0:T(8,128)(2,1)S(1)} %select_convert_fusion.ids_ref, f32[512,1280]{1,0:T(8,128)S(1)} %copy-done.1, ...), custom_call_target="tpu_custom_call" | custom-call | tf_op jit(solution)/shard_map/exchange_and_gather/pallas_call | solution.py:241
  120.1 1.5 %copy.14 = f32[512,1280]{1,0:T(8,128)} copy(f32[512,1280]{1,0:T(8,128)S(1)} %get-tuple-element.18) | data formatting | bytes 5242880
  121.6 1.5 %copy.15 = f32[512,1280]{1,0:T(8,128)} copy(f32[512,1280]{1,0:T(8,128)S(1)} %get-tuple-element.19) | data formatting | bytes 5242880
  123.1 1.5 %copy.16 = f32[512,1280]{1,0:T(8,128)} copy(f32[512,1280]{1,0:T(8,128)S(1)} %get-tuple-element.20) | data formatting | bytes 5242880
  124.5 2.4 %copy.17 = bf16[512,5120]{1,0:T(8,128)(2,1)} copy(bf16[512,5120]{1,0:T(8,128)(2,1)S(1)} %get-tuple-element.21) | data formatting | bytes 10485760
  (2 shorter events, 0.0 us)
Async XLA Ops:
  0.6 2.6 %copy-start = (bf16[256,5120]{1,0:T(8,128)(2,1)S(1)}, bf16[256,5120]{1,0:T(8,128)(2,1)}, u32[]{:S(2)}) copy-start(bf16[256,5120]{1,0:T(8,128)(2,1)} %param.8) | copy-start | bytes 7864324
  3.2 1.8 %copy-start.1 = (f32[512,1280]{1,0:T(8,128)S(1)}, f32[512,1280]{1,0:T(8,128)}, u32[]{:S(2)}) copy-start(f32[512,1280]{1,0:T(8,128)} %master_hbm.1) | copy-start | bytes 7864324
  4.9 1.7 %copy-start.2 = (f32[512,1280]{1,0:T(8,128)S(1)}, f32[512,1280]{1,0:T(8,128)}, u32[]{:S(2)}) copy-start(f32[512,1280]{1,0:T(8,128)} %first_hbm.1) | copy-start | bytes 7864324
  6.6 1.7 %copy-start.3 = (f32[512,1280]{1,0:T(8,128)S(1)}, f32[512,1280]{1,0:T(8,128)}, u32[]{:S(2)}) copy-start(f32[512,1280]{1,0:T(8,128)} %second_hbm.1) | copy-start | bytes 7864324

commit v4 on v3

--- a/solution.py
+++ b/solution.py
@@ -266,7 +266,7 @@
             collective_id=0, has_side_effects=True, vmem_limit_bytes=20 * 2**20
         ),
         name="exchange_and_gather",
-    )(outgoing, ids, master, first, second)
+    )(outgoing, ids, *(pltpu.with_memory_space_constraint(x, pltpu.HBM) for x in (master, first, second)))
 
 
 def copy_kernel(src_ref, dst_ref):

time: 127 us -> 122 us (0.961)
  local copies, waits for them, and re-layouts: 11.5 us -> 6.92 us
    unnamed x12 -> x6, local copies, waits for them, and re-layouts: 11.4 us -> 6.84 us
where the time goes in v4:
time: 122 us
  Pallas kernels  111 us (91%)
  local copies, waits for them, and re-layouts  6.92 us (6%)
  other arithmetic  1.72 us (1%)
  between operations  1.49 us (1%)
    pallas_call x1, Pallas kernels, exchange_and_gather(): pl.pallas_call(functools.partial(step_kernel, groups, owners, kept), out_...  111 us
    unnamed x6, local copies, waits for them, and re-layouts  6.84 us

profile of v4, /device:TPU:0, one launch (start us, length us, event | category | flops | bytes accessed | tf_op | source)
XLA Modules:
  0.0 121.9 jit_solution(15947775076070468505)
XLA Ops:
  0.6 0.0 copy-start
  1.5 0.7 and_select_fusion
  2.1 0.1 convert_reduce_fusion
  2.3 0.7 add_select_fusion.2
  3.0 0.1 select_reduce_fusion
  3.1 0.1 reduce_max.12
  3.2 0.1 select_convert_fusion.ids_ref
  3.3 0.0 copy-done
  3.3 0.6 convolution_convert_fusion.out_ref
  3.9 111.2 %exchange_and_gather.1 = (bf16[512,5120]{1,0:T(8,128)(2,1)S(1)}, f32[512,1280]{1,0:T(8,128)S(1)}, f32[512,1280]{1,0:T(8,128)S(1)}, f32[512,1280]{1,0:T(8,128)S(1)}) custom-call(bf16[64,5120]{1,0:T(8,128)(2,1)S(1)} %convolution_convert_fusion.out_ref, bf16[8,8,128]{2,1,0:T(8,128)(2,1)S(1)} %select_convert_fusion.ids_ref, f32[512,1280]{1,0:T(8,128)} %master_hbm.1, ...), custom_call_target="tpu_custom_call" | custom-call | tf_op jit(solution)/shard_map/exchange_and_gather/pallas_call | solution.py:241
  115.0 1.5 %copy.14 = f32[512,1280]{1,0:T(8,128)} copy(f32[512,1280]{1,0:T(8,128)S(1)} %get-tuple-element.18) | data formatting | bytes 5242880
  116.5 1.5 %copy.15 = f32[512,1280]{1,0:T(8,128)} copy(f32[512,1280]{1,0:T(8,128)S(1)} %get-tuple-element.19) | data formatting | bytes 5242880
  118.0 1.5 %copy.16 = f32[512,1280]{1,0:T(8,128)} copy(f32[512,1280]{1,0:T(8,128)S(1)} %get-tuple-element.20) | data formatting | bytes 5242880
  119.5 2.4 %copy.17 = bf16[512,5120]{1,0:T(8,128)(2,1)} copy(bf16[512,5120]{1,0:T(8,128)(2,1)S(1)} %get-tuple-element.21) | data formatting | bytes 10485760
  (2 shorter events, 0.0 us)
Async XLA Ops:
  0.6 2.6 %copy-start = (bf16[256,5120]{1,0:T(8,128)(2,1)S(1)}, bf16[256,5120]{1,0:T(8,128)(2,1)}, u32[]{:S(2)}) copy-start(bf16[256,5120]{1,0:T(8,128)(2,1)} %param.8) | copy-start | bytes 7864324

commit v5 on v4

--- a/solution.py
+++ b/solution.py
@@ -11,7 +11,7 @@
 CAP = 8
 LANES = 128
 CHUNKS = 8
-KEPT = 8
+KEPT = 6
 MESH = pl.DeviceIdType.MESH
 
 
@@ -269,20 +269,23 @@
     )(outgoing, ids, *(pltpu.with_memory_space_constraint(x, pltpu.HBM) for x in (master, first, second)))
 
 
-def copy_kernel(src_ref, dst_ref):
-    dst_ref[...] = src_ref[...]
+def copy_kernel(src_ref, dst_ref, sem):
+    copy = pltpu.make_async_copy(src_ref, dst_ref, sem)
+    copy.start()
+    copy.wait()
 
 
 def fresh_copy(table):
     rows, width = table.shape
-    block = pl.BlockSpec((rows // CHUNKS, width), lambda i: (i, 0))
+    anywhere = pl.BlockSpec(memory_space=pl.ANY)
     return pl.pallas_call(
         copy_kernel,
-        out_shape=jax.ShapeDtypeStruct(table.shape, table.dtype),
-        grid=(CHUNKS,),
-        in_specs=[block],
-        out_specs=block,
+        out_shape=pltpu.HBM(table.shape, table.dtype),
+        in_specs=[anywhere],
+        out_specs=anywhere,
+        scratch_shapes=[pltpu.SemaphoreType.DMA],
         cost_estimate=pl.CostEstimate(flops=0, bytes_accessed=4 * rows * width, transcendentals=0),
+        compiler_params=pltpu.CompilerParams(vmem_limit_bytes=2**20),
         name="fresh_copy",
     )(table)
 
@@ -304,10 +307,11 @@
     return pl.pallas_call(
         functools.partial(patch_kernel, groups),
         out_shape=jax.ShapeDtypeStruct(table.shape, table.dtype),
-        in_specs=[pl.BlockSpec(memory_space=pltpu.VMEM), pl.BlockSpec(memory_space=pl.ANY)],
+        in_specs=[pl.BlockSpec(memory_space=pl.ANY), pl.BlockSpec(memory_space=pl.ANY)],
         out_specs=pl.BlockSpec(memory_space=pl.ANY),
         scratch_shapes=[pltpu.SemaphoreType.DMA],
         input_output_aliases={1: 0},
+        compiler_params=pltpu.CompilerParams(vmem_limit_bytes=2**20),
         name="patch",
     )(tail, table)
 

time: 122 us -> 121 us (level)
  Pallas kernels: 111 us -> 107 us
  waiting for transfers between devices: 0 us -> 3.47 us
  local copies, waits for them, and re-layouts: 6.92 us -> 4.6 us
  starting transfers between devices: 0 us -> 1.29 us
    pallas_call x1, Pallas kernels: 111 us -> 104 us  [exchange_and_gather(): pl.pallas_call(functools.partial(step_kernel, groups, owners, kept), out_...]
    ppermute x0 -> x1, waiting for transfers between devices: none -> 3.47 us  [body(): tail = lax.ppermute(tail, 'dp', [(1, 0), (groups - 2, groups - 1)])]
    pallas_call x0 -> x2, Pallas kernels: none -> 3.1 us  [the longest x1 2.37 us: fresh_copy(): pl.pallas_call(copy_kernel, out_shape=pltpu.HBM(table.shape, table.dtype)...]
    unnamed x6 -> x5, local copies, waits for them, and re-layouts: 6.84 us -> 4.49 us
    ppermute x0 -> x1, starting transfers between devices: none -> 1.29 us  [body(): tail = lax.ppermute(tail, 'dp', [(1, 0), (groups - 2, groups - 1)])]
  transfers between devices with their start and end apart: 0 -> 1, of which waited for: 0 -> 1; matrix products, arithmetic and copies ran while one was open for 0% -> 4% of each run, Pallas kernels for 0% -> 2%
where the time goes in v5:
time: 121 us; the launch traced here: 120 us
  Pallas kernels  107 us (88%)
  local copies, waits for them, and re-layouts  4.6 us (4%)
  waiting for transfers between devices  3.47 us (3%)
  other arithmetic  1.71 us (1%)
  between operations  1.52 us (1%)
  starting transfers between devices  1.29 us (1%)
    pallas_call x1, Pallas kernels, exchange_and_gather(): pl.pallas_call(functools.partial(step_kernel, groups, owners, kept), out_...  104 us
    unnamed x5, local copies, waits for them, and re-layouts  4.49 us
    ppermute x1, waiting for transfers between devices, body(): tail = lax.ppermute(tail, 'dp', [(1, 0), (groups - 2, groups - 1)])  3.47 us
  transfers between devices with their start and end apart: 1, of which 1 were waited for; matrix products, arithmetic and copies ran while one was open for 4% of the time, Pallas kernels for 2%

profile of v5, /device:TPU:0, one launch (start us, length us, event | category | flops | bytes accessed | tf_op | source)
XLA Modules:
  0.0 120.4 jit_solution(6213041067089835691)
XLA Ops:
  0.6 0.0 copy-start
  1.5 0.7 and_select_fusion
  2.2 0.1 convert_reduce_fusion
  2.3 0.7 add_select_fusion.2
  3.0 0.1 select_reduce_fusion
  3.1 0.1 reduce_max.12
  3.2 0.0 copy-done
  3.2 0.6 convolution_convert_fusion.out_ref
  3.8 0.1 select_convert_fusion.ids_ref
  3.9 104.1 %exchange_and_gather.1 = (bf16[512,5120]{1,0:T(8,128)(2,1)S(1)}, f32[512,1280]{1,0:T(8,128)S(1)}, f32[512,1280]{1,0:T(8,128)S(1)}, f32[512,1280]{1,0:T(8,128)S(1)}) custom-call(bf16[64,5120]{1,0:T(8,128)(2,1)S(1)} %convolution_convert_fusion.out_ref, bf16[8,8,128]{2,1,0:T(8,128)(2,1)S(1)} %select_convert_fusion.ids_ref, f32[512,1280]{1,0:T(8,128)} %master_hbm.1, ...), custom_call_target="tpu_custom_call" | custom-call | tf_op jit(solution)/shard_map/exchange_and_gather/pallas_call | solution.py:241
  108.1 1.3 %collective-permute-start = (bf16[128,1280]{1,0:T(8,128)(2,1)S(1)}, bf16[128,1280]{1,0:T(8,128)(2,1)S(1)}, u32[]{:S(2)}, u32[]{:S(2)}) collective-permute-start(bf16[128,1280]{1,0:T(8,128)(2,1)S(1)} %constant_dynamic-slice_fusion), channel_id=1, source_target_pairs={{8,0},{16,24},{9,1},{17,25},{10,2},{18,26},{11,3},{19,27},{12,4},{... | collective-permute-start | bytes 983048 | tf_op jit(solution)/shard_map/ppermute | solution.py:352
  109.4 2.4 %fresh_copy.1.old_ref = bf16[512,5120]{1,0:T(8,128)(2,1)} custom-call(bf16[512,5120]{1,0:T(8,128)(2,1)S(1)} %get-tuple-element.11.src_ref), custom_call_target="tpu_custom_call" | custom-call | bytes 10485760 | tf_op jit(solution)/shard_map/fresh_copy/pallas_call | solution.py:281
  111.7 1.5 %copy.15 = f32[512,1280]{1,0:T(8,128)} copy(f32[512,1280]{1,0:T(8,128)S(1)} %get-tuple-element.18) | data formatting | bytes 5242880
  113.2 1.5 %copy.16 = f32[512,1280]{1,0:T(8,128)} copy(f32[512,1280]{1,0:T(8,128)S(1)} %get-tuple-element.19) | data formatting | bytes 5242880
  114.7 1.5 %copy.17 = f32[512,1280]{1,0:T(8,128)} copy(f32[512,1280]{1,0:T(8,128)S(1)} %get-tuple-element.20) | data formatting | bytes 5242880
  116.2 3.5 %collective-permute-done.tail_ref = bf16[128,1280]{1,0:T(8,128)(2,1)S(1)} collective-permute-done((bf16[128,1280]{1,0:T(8,128)(2,1)S(1)}, bf16[128,1280]{1,0:T(8,128)(2,1)S(1)}, u32[]{:S(2)}, u32[]{:S(2)}) %collective-permute-start) | collective-permute-done | bytes 327712 | tf_op jit(solution)/shard_map/ppermute | solution.py:352
  119.7 0.7 patch.1
  (3 shorter events, 0.1 us)
Async XLA Ops:
  0.6 2.6 %copy-start = (bf16[256,5120]{1,0:T(8,128)(2,1)S(1)}, bf16[256,5120]{1,0:T(8,128)(2,1)}, u32[]{:S(2)}) copy-start(bf16[256,5120]{1,0:T(8,128)(2,1)} %param.8) | copy-start | bytes 7864324
  108.1 11.6 %collective-permute-start = (bf16[128,1280]{1,0:T(8,128)(2,1)S(1)}, bf16[128,1280]{1,0:T(8,128)(2,1)S(1)}, u32[]{:S(2)}, u32[]{:S(2)}) collective-permute-start(bf16[128,1280]{1,0:T(8,128)(2,1)S(1)} %constant_dynamic-slice_fusion), channel_id=1, source_target_pairs={{8,0},{16,24},{9,1},{17,25},{10,2},{18,26},{11,3},{19,27},{12,4},{... | collective-permute-start | bytes 983048 | tf_op jit(solution)/shard_map/ppermute | solution.py:352
